TPU v7x, 256 devices: a whole 4x4x8 slice. The times are simulated.
256 devices in a mesh: dp: 2 (over y_hi), fsdp: 16 (over x, y_lo, core), tensor: 8 (over z).
Axes of the slice: x: 4, y: 4 (y_hi: 2, y_lo: 2; y = y_hi * 2 + y_lo), z: 8, core: 2. Of those that a mesh axis runs over, the one named last changes fastest.
Arguments:
- activations: bfloat16 [4096, 8192], P(('dp', 'fsdp'), 'tensor'), may hold values from -6 to 6
- cotangent: bfloat16 [4096, 8192], P(('dp', 'fsdp'), 'tensor'), may hold values from -6 to 6
- up_tiles: bfloat16 [1024, 128, 128], P(('fsdp', 'tensor')), may hold values from -0.1875 to 0.1875
- down_tiles: bfloat16 [1024, 128, 128], P(('fsdp', 'tensor')), may hold values from -0.125 to 0.125
- up_rows: int32 [128, 8], P(None, 'tensor'), may hold values from 0 to 63, as said below
- up_cols: int32 [128, 8], P(None, 'tensor'), may hold values from 0 to 15, as said below
- down_rows: int32 [128, 8], P(None, 'tensor'), may hold values from 0 to 15, as said below
- down_cols: int32 [128, 8], P(None, 'tensor'), may hold values from 0 to 63, as said below
Outputs:
- output: bfloat16 [4096, 8192], P(('dp', 'fsdp'), 'tensor')
- input_grad: bfloat16 [4096, 8192], P(('dp', 'fsdp'), 'tensor')
- up_grad: float32 [1024, 128, 128], P(('fsdp', 'tensor'))
- down_grad: float32 [1024, 128, 128], P(('fsdp', 'tensor'))
Inputs may be any that keep to these rules, and one draw needn't show every extreme that they name: `up_rows`: within a column, the up tiles of one hidden-unit block name distinct feature blocks. `up_cols`: every value occurs exactly 8 times in each column. `down_rows`: every value occurs exactly 8 times in each column. `down_cols`: within a column, the down tiles of one hidden-unit block name distinct feature blocks.
All inputs are finite; a program needn't handle non-finite values.
Results may differ from a plain program's by a relative error of at most 0.018.
Values may be sent and summed in bfloat16 or wider, within the bound.
No kernel may reach another device: no remote copies, remote signals or barrier semaphores. Data moves between devices by JAX's collectives and lax.ppermute only.
A program may use at most 128 MiB of HBM per device.

v0:
```python
import jax
import jax.numpy as jnp
from jax import lax
from jax.sharding import PartitionSpec as P

D = 8192
FF = 16384
inv_root_two = 0.7071067811865476
inv_root_tau = 0.3989422804014327


def gelu_parts(values):
    normal_cdf = 0.5 * (1.0 + jax.scipy.special.erf(values * inv_root_two))
    density = inv_root_tau * jnp.exp(-0.5 * values * values)
    return (values * normal_cdf, normal_cdf + values * density)


def grouped_pick(acting, far_index, hidden_blocks, block_size):
    rows_here = acting.shape[0]
    picked = acting.reshape(rows_here, -1, block_size)[:, far_index]
    return picked.reshape(rows_here, hidden_blocks, -1, block_size)


def add_far(product, far_index, model_blocks):
    rows_here = product.shape[0]
    block_size = product.shape[-1]
    flat = product.reshape(rows_here, -1, block_size)
    summed = (
        jnp.zeros((rows_here, model_blocks, block_size), jnp.float32).at[:, far_index].add(flat)
    )
    return summed.reshape(rows_here, model_blocks * block_size)


def grouped_tiles(tiles, order, hidden_blocks):
    block_size = tiles.shape[1]
    return tiles[order].reshape(hidden_blocks, -1, block_size, block_size)


def body(activations, cotangent, up_tiles, down_tiles, up_rows, up_cols, down_rows, down_cols):
    block_size = up_tiles.shape[1]
    hidden_blocks = FF // (block_size * lax.axis_size("tensor"))
    model_blocks = D // block_size
    up_order = jnp.argsort(up_cols[:, 0], stable=True)
    down_order = jnp.argsort(down_rows[:, 0], stable=True)
    up_back = jnp.argsort(up_order)
    down_back = jnp.argsort(down_order)
    up_far = up_rows[:, 0][up_order]
    down_far = down_cols[:, 0][down_order]
    full_input = lax.all_gather(activations, "tensor", axis=1, tiled=True)
    input_pick = grouped_pick(full_input, up_far, hidden_blocks, block_size)
    up_whole = lax.all_gather(up_tiles, "fsdp", axis=0, tiled=True)
    up_sorted = grouped_tiles(up_whole, up_order, hidden_blocks)
    pre_act = jnp.einsum(
        "thkb,hkbc->thc", input_pick, up_sorted, preferred_element_type=jnp.float32
    )
    gelu_out, gelu_slope = gelu_parts(pre_act)
    hidden = gelu_out.astype(jnp.bfloat16)
    down_whole = lax.all_gather(down_tiles, "fsdp", axis=0, tiled=True)
    down_sorted = grouped_tiles(down_whole, down_order, hidden_blocks)
    out_product = jnp.einsum(
        "thb,hkbc->thkc", hidden, down_sorted, preferred_element_type=jnp.float32
    )
    partial_out = add_far(out_product, down_far, model_blocks)
    output = lax.psum_scatter(
        partial_out.astype(jnp.bfloat16), "tensor", scatter_dimension=1, tiled=True
    )
    full_cotangent = lax.all_gather(cotangent, "tensor", axis=1, tiled=True)
    cot_pick = grouped_pick(full_cotangent, down_far, hidden_blocks, block_size)
    hidden_grad = jnp.einsum(
        "thkc,hkbc->thb", cot_pick, down_sorted, preferred_element_type=jnp.float32
    )
    pre_grad = (hidden_grad * gelu_slope).astype(jnp.bfloat16)
    in_product = jnp.einsum(
        "thc,hkbc->thkb", pre_grad, up_sorted, preferred_element_type=jnp.float32
    )
    partial_in = add_far(in_product, up_far, model_blocks)
    input_grad = lax.psum_scatter(
        partial_in.astype(jnp.bfloat16), "tensor", scatter_dimension=1, tiled=True
    )
    up_grouped = jnp.einsum(
        "thkb,thc->hkbc", input_pick, pre_grad, preferred_element_type=jnp.float32
    )
    down_grouped = jnp.einsum(
        "thb,thkc->hkbc", hidden, cot_pick, preferred_element_type=jnp.float32
    )
    up_rounded = up_grouped.astype(jnp.bfloat16).reshape(-1, block_size, block_size)
    down_rounded = down_grouped.astype(jnp.bfloat16).reshape(-1, block_size, block_size)
    up_term = up_rounded[up_back].astype(jnp.float32)
    down_term = down_rounded[down_back].astype(jnp.float32)
    up_part, down_part = (
        lax.psum_scatter(
            up_term.astype(jnp.bfloat16), "fsdp", scatter_dimension=0, tiled=True
        ).astype(jnp.float32),
        lax.psum_scatter(
            down_term.astype(jnp.bfloat16), "fsdp", scatter_dimension=0, tiled=True
        ).astype(jnp.float32),
    )
    up_grad, down_grad = (
        lax.psum(up_part.astype(jnp.bfloat16), "dp").astype(jnp.float32),
        lax.psum(down_part.astype(jnp.bfloat16), "dp").astype(jnp.float32),
    )
    return (output, input_grad, up_grad, down_grad)


def solution(mesh):
    in_specs = (
        P(("dp", "fsdp"), "tensor"),
        P(("dp", "fsdp"), "tensor"),
        P(("fsdp", "tensor"), None, None),
        P(("fsdp", "tensor"), None, None),
        P(None, "tensor"),
        P(None, "tensor"),
        P(None, "tensor"),
        P(None, "tensor"),
    )
    out_specs = (
        P(("dp", "fsdp"), "tensor"),
        P(("dp", "fsdp"), "tensor"),
        P(("fsdp", "tensor"), None, None),
        P(("fsdp", "tensor"), None, None),
    )
    return jax.shard_map(body, mesh=mesh, in_specs=in_specs, out_specs=out_specs, check_vma=False)
```

profile of v0, /device:TPU:1, one launch (start us, length us, event | category | flops | bytes accessed | tf_op | source)
XLA Modules:
  0.0 480.6 jit_solution(9236470539080875752)
XLA Ops:
  7.2 1.8 copy.58
  9.1 1.8 copy.65
  11.0 0.7 all-gather.7.cloned.1.call-update
  11.7 0.5 all-gather.5.cloned.1.call-update
  12.3 3.2 sort.63
  15.5 2.5 sort.64
  18.0 1.2 gather_fusion.3
  19.3 3.2 sort.62
  22.5 1.6 gather_fusion
  24.1 28.0 %all-gather.9.cloned.1.call-done = bf16[128,8192]{0,1:T(8,128)(2,1)} async-done(((bf16[128,1024]{0,1:T(8,128)(2,1)}), bf16[128,8192]{0,1:T(8,128)(2,1)}) %all-gather.9.cloned.1.call-update) | async-done | bytes 2097168 | tf_op jit(solution)/shard_map/all_gather | solution.py:49
  52.1 3.2 copy.59
  55.3 39.0 %all-gather.11.cloned.1.call-done = bf16[128,8192]{0,1:T(8,128)(2,1)} async-done(((bf16[128,1024]{0,1:T(8,128)(2,1)}), bf16[128,8192]{0,1:T(8,128)(2,1)}) %all-gather.11.cloned.1.call-update) | async-done | bytes 2097168 | tf_op jit(solution)/shard_map/all_gather | solution.py:67
  94.3 4.1 copy.66
  98.4 3.0 gather_fusion.4
  101.4 4.6 gather_fusion.5
  106.0 32.7 %all-gather.7.cloned.1.call-done = bf16[128,128,128]{2,1,0:T(8,128)(2,1)} async-done(((bf16[8,128,128]{2,1,0:T(8,128)(2,1)}), bf16[128,128,128]{2,1,0:T(8,128)(2,1)}) %all-gather.7.cloned.1.call-update) | async-done | bytes 4194320 | tf_op jit(solution)/shard_map/all_gather | solution.py:51
  138.7 5.2 %gather_fusion.2 = bf16[128,128,128]{2,1,0:T(8,128)(2,1)} fusion(bf16[128,128,128]{2,1,0:T(8,128)(2,1)} %all-gather.7.cloned.1.call-done, s32[1024]{0:T(1024)S(1)} %pad_clamp_fusion.4), kind=kCustom, calls=%fused_computation.2 | custom fusion | bytes 8389120 | tf_op jit(solution)/shard_map/gather | solution.py:36
  143.9 4.8 convolution_bitcast_fusion.1
  148.7 31.7 %all-gather.5.cloned.1.call-done = bf16[128,128,128]{2,1,0:T(8,128)(2,1)} async-done(((bf16[8,128,128]{2,1,0:T(8,128)(2,1)}), bf16[128,128,128]{2,1,0:T(8,128)(2,1)}) %all-gather.5.cloned.1.call-update) | async-done | bytes 4194320 | tf_op jit(solution)/shard_map/all_gather | solution.py:58
  180.5 5.2 %gather_fusion.1 = bf16[128,128,128]{2,1,0:T(8,128)(2,1)} fusion(bf16[128,128,128]{2,1,0:T(8,128)(2,1)} %all-gather.5.cloned.1.call-done, s32[1024]{0:T(1024)S(1)} %pad_clamp_fusion.5), kind=kCustom, calls=%fused_computation.1 | custom fusion | bytes 8389120 | tf_op jit(solution)/shard_map/gather | solution.py:36
  185.7 5.0 %fusion.2 = bf16[128,16,128,1]{0,2,3,1:T(8,128)(2,1)S(1)} fusion(bf16[16,8,128,128]{3,2,1,0:T(8,128)(2,1)} %bitcast.84, bf16[128,16,8,128]{3,0,2,1:T(8,128)(2,1)} %bitcast.86, f32[128,16,128]{0,2,1:T(8,128)S(1)} %convolution_bitcast_fusion.1), kind=kOutput, calls=%fused_computation.17 | convolution fusion | flops 539492352 | bytes 9961472 | tf_op jit(solution)/shard_map/thkc,hkbc->thb/dot_general | solution.py:69
  190.7 3.3 convolution_convert_fusion.1
  194.0 5.2 %gather_fusion.6 = bf16[128,128,128]{2,1,0:T(8,128)(2,1)} fusion(bf16[128,128,128]{2,1,0:T(8,128)(2,1)} %bitcast.88, s32[1024]{0:T(1024)S(1)} %pad_clamp_fusion.1), kind=kCustom, calls=%fused_computation.6 | custom fusion | bytes 8389120 | tf_op jit(solution)/shard_map/gather | solution.py:88
  199.2 0.2 reduce-scatter.11.cloned.1.call-start
  199.5 2.5 sort.65
  202.0 5.6 %convolution_convert_fusion = bf16[16,8,128,128]{3,2,1,0:T(8,128)(2,1)} fusion(bf16[128,16,8,128]{3,0,2,1:T(8,128)(2,1)} %bitcast.87, f32[128,16,128]{0,2,1:T(8,128)S(1)} %convolution_bitcast_fusion.1), kind=kOutput, calls=%fused_computation.10 | convolution fusion | flops 540278784 | bytes 9437184 | tf_op jit(solution)/shard_map/thb,thkc->hkbc/dot_general | solution.py:83
  207.6 6.4 %copy.74 = bf16[128,128,128]{2,1,0:T(8,128)(2,1)} copy(bf16[128,128,128]{1,2,0:T(8,128)(2,1)} %bitcast.89) | data formatting | bytes 8388608 | tf_op jit(solution)/shard_map/reshape | solution.py:87
  214.0 5.3 %gather_fusion.7 = bf16[128,128,128]{2,1,0:T(8,128)(2,1)} fusion(bf16[128,128,128]{2,1,0:T(8,128)(2,1)} %copy.74, s32[1024]{0:T(1024)S(1)} %pad_clamp_fusion), kind=kCustom, calls=%fused_computation.7 | custom fusion | bytes 8389120 | tf_op jit(solution)/shard_map/gather | solution.py:89
  219.4 6.7 %fusion.13 = f32[16,8,128,128]{3,2,1,0:T(8,128)} fusion(bf16[16,8,128,128]{3,2,1,0:T(8,128)(2,1)} %bitcast.77, bf16[128,16,128,1]{0,2,3,1:T(8,128)(2,1)S(1)} %fusion.2), kind=kOutput, calls=%fused_computation.40 | convolution fusion | flops 536870912 | bytes 13107200 | tf_op jit(solution)/shard_map/thc,hkbc->thkb/dot_general | solution.py:73
  226.1 9.0 %copy.68 = f32[128,128,128]{2,0,1:T(8,128)} copy(f32[128,128,128]{0,2,1:T(8,128)} %bitcast.82) | data formatting | bytes 16777216 | tf_op jit(solution)/shard_map/reshape | solution.py:27
  235.1 2.5 broadcast.42.clone.1
  237.6 26.7 %scatter_fusion.1 = f32[128,64,128]{2,0,1:T(8,128)} fusion(f32[128,64,128]{2,0,1:T(8,128)} %broadcast.42.clone.1, s32[128]{0:T(128)S(1)} %fusion.9, f32[128,128,128]{2,1,0:T(8,128)} %bitcast.81), kind=kCustom, calls=%fused_computation.9 | custom fusion | flops 2097152 | bytes 25166336 | tf_op jit(solution)/shard_map/scatter-add | solution.py:29
  264.3 2.6 convert_element_type.45
  266.9 2.9 copy.69
  270.0 6.8 %fusion.11 = f32[16,8,128,128]{3,2,1,0:T(8,128)} fusion(bf16[16,8,128,128]{3,2,1,0:T(8,128)(2,1)} %bitcast.85, f32[128,16,128]{0,2,1:T(8,128)S(1)} %convolution_bitcast_fusion.1), kind=kOutput, calls=%fused_computation.39 | convolution fusion | flops 538181632 | bytes 13631488 | tf_op jit(solution)/shard_map/thb,hkbc->thkc/dot_general | solution.py:60
  276.7 9.0 %copy.63 = f32[128,128,128]{2,0,1:T(8,128)} copy(f32[128,128,128]{0,2,1:T(8,128)} %bitcast.83) | data formatting | bytes 16777216 | tf_op jit(solution)/shard_map/reshape | solution.py:27
  285.8 2.5 broadcast.42.clone
  288.2 26.9 %scatter_fusion = f32[128,64,128]{2,0,1:T(8,128)} fusion(f32[128,64,128]{2,0,1:T(8,128)} %broadcast.42.clone, s32[128]{0:T(128)S(1)} %fusion.8, f32[128,128,128]{2,1,0:T(8,128)} %bitcast.80), kind=kCustom, calls=%fused_computation.8 | custom fusion | flops 2097152 | bytes 25166336 | tf_op jit(solution)/shard_map/scatter-add | solution.py:29
  315.1 2.6 convert_element_type.42
  317.7 2.9 copy.64
  320.7 16.4 %reduce-scatter.11.cloned.1.call-done = bf16[8,128,128]{2,1,0:T(8,128)(2,1)} async-done(((bf16[128,128,128]{2,1,0:T(8,128)(2,1)}), bf16[8,128,128]{2,1,0:T(8,128)(2,1)}) %reduce-scatter.11.cloned.1.call-update) | async-done | bytes 262160 | tf_op jit(solution)/shard_map/reduce_scatter | solution.py:94
  337.1 42.2 %reduce-scatter.7.cloned.1.call-done = bf16[128,1024]{0,1:T(8,128)(2,1)} async-done(((bf16[128,8192]{0,1:T(8,128)(2,1)}), bf16[128,1024]{0,1:T(8,128)(2,1)}) %reduce-scatter.7.cloned.1.call-update) | async-done | bytes 262160 | tf_op jit(solution)/shard_map/reduce_scatter | solution.py:77
  379.4 1.8 copy.76
  381.1 41.9 %reduce-scatter.5.cloned.1.call-done = bf16[128,1024]{0,1:T(8,128)(2,1)} async-done(((bf16[128,8192]{0,1:T(8,128)(2,1)}), bf16[128,1024]{0,1:T(8,128)(2,1)}) %reduce-scatter.5.cloned.1.call-update) | async-done | bytes 262160 | tf_op jit(solution)/shard_map/reduce_scatter | solution.py:64
  423.0 1.8 copy.75
  424.8 45.7 %all-reduce.3.cloned.1.call-done = (bf16[8,128,128]{2,1,0:T(8,128)(2,1)}, bf16[8,128,128]{2,1,0:T(8,128)(2,1)}) async-done(((bf16[8,128,128]{2,1,0:T(8,128)(2,1)}, bf16[8,128,128]{2,1,0:T(8,128)(2,1)}), (bf16[8,128,128]{2,1,0:T(8,128)(2,1)}, bf16[8,128,128]{2,1,0:T(8,128)(2,1)})) %all-reduce.3.cloned.1.call-update) | async-done | bytes 524304 | tf_op jit(solution)/shard_map/psum | solution.py:99
  470.5 1.8 convert_element_type.48
  472.3 1.8 convert_element_type.51
  (38 shorter events, 0.5 us)
Async XLA Ops:
  7.2 10.9 %copy-start = (s32[128,1]{0,1:T(1,128)S(1)}, s32[128,1]{0,1:T(1,128)}, u32[]{:S(2)}) copy-start(s32[128,1]{0,1:T(1,128)} %param.12) | copy-start | bytes 1540
  7.2 44.9 %all-gather.9.cloned.1.call-start = ((), (), s32[]{:S(2)}) async-start(), calls=%async_computation.6 | async-start | bytes 2359296 | tf_op jit(solution)/shard_map/all_gather | solution.py:49
  9.0 85.3 %all-gather.11.cloned.1.call-start = ((), (), s32[]{:S(2)}) async-start(), calls=%async_computation.8 | async-start | bytes 2359296 | tf_op jit(solution)/shard_map/all_gather | solution.py:67
  10.9 127.8 %all-gather.7.cloned.1.call-start = ((), (), s32[]{:S(2)}) async-start(), calls=%async_computation.5 | async-start | bytes 4456448 | tf_op jit(solution)/shard_map/all_gather | solution.py:51
  11.7 168.8 %all-gather.5.cloned.1.call-start = ((), (), s32[]{:S(2)}) async-start(), calls=%async_computation.4 | async-start | bytes 4456448 | tf_op jit(solution)/shard_map/all_gather | solution.py:58
  12.2 308.5 %reduce-scatter.9.cloned.1.call-start = ((), (), s32[]{:S(2)}) async-start(), calls=%async_computation.10 | async-start | bytes 4456448 | tf_op jit(solution)/shard_map/reduce_scatter | solution.py:91
  185.7 5.0 %copy-start.2 = (bf16[128,128,128]{2,1,0:T(8,128)(2,1)S(1)}, bf16[128,128,128]{2,1,0:T(8,128)(2,1)}, u32[]{:S(2)}) copy-start(bf16[128,128,128]{2,1,0:T(8,128)(2,1)} %gather_fusion.4) | copy-start | bytes 12582916
  199.2 137.9 %reduce-scatter.11.cloned.1.call-start = ((), (), s32[]{:S(2)}) async-start(), calls=%async_computation.11 | async-start | bytes 4456448 | tf_op jit(solution)/shard_map/reduce_scatter | solution.py:94
  219.4 160.0 %reduce-scatter.7.cloned.1.call-start = ((), (), s32[]{:S(2)}) async-start(), calls=%async_computation.9 | async-start | bytes 2359296 | tf_op jit(solution)/shard_map/reduce_scatter | solution.py:77
  269.9 153.1 %reduce-scatter.5.cloned.1.call-start = ((), (), s32[]{:S(2)}) async-start(), calls=%async_computation.7 | async-start | bytes 2359296 | tf_op jit(solution)/shard_map/reduce_scatter | solution.py:64
  315.1 158.9 %copy-start.1 = (s32[128,1]{0,1:T(1,128)S(1)}, s32[128,1]{0,1:T(1,128)}, u32[]{:S(2)}) copy-start(s32[128,1]{0,1:T(1,128)} %param.12) | copy-start | bytes 1540
  320.7 149.9 %all-reduce.3.cloned.1.call-start = ((), (), s32[]{:S(2)}) async-start(), calls=%async_computation.12 | async-start | bytes 1048576 | tf_op jit(solution)/shard_map/psum | solution.py:99
Sparse Core Ops, SparseCore 0:
  10.4 41.6 all-gather.8
  54.5 39.8 all-gather.10
  96.2 42.5 all-gather.6
  140.4 39.9 all-gather.4
  199.3 66.5 reduce-scatter.8
  268.4 68.6 reduce-scatter.10
  339.7 39.6 reduce-scatter.6
  381.9 41.0 reduce-scatter.4
  425.7 44.8 all-reduce.2
where the time goes:
time: 482 us; the launch traced here: 481 us
  waiting for transfers between devices  279 us (58%)
  local copies, waits for them, and re-layouts  81.1 us (17%)
  other arithmetic  73.8 us (15%)
  matrix products  32.2 us (7%)
  between operations  14 us (3%)
    scatter-add x2, other arithmetic, add_far(): jnp.zeros((rows_here, model_blocks, block_size), jnp.float32)  53.6 us
    psum x1, waiting for transfers between devices, body(): lax.psum(up_part.astype(jnp.bfloat16), 'dp').astype(jnp.float32)  45.7 us
    reduce_scatter x1, waiting for transfers between devices, body(): lax.psum_scatter(partial_in.astype(jnp.bfloat16), 'tensor', scatter_dimen...  42.2 us
    reduce_scatter x1, waiting for transfers between devices, body(): lax.psum_scatter(partial_out.astype(jnp.bfloat16), 'tensor', scatter_dime...  41.9 us
    all_gather x1, waiting for transfers between devices, body(): full_cotangent = lax.all_gather(cotangent, 'tensor', axis=1, tiled=True)  39 us
    all_gather x1, waiting for transfers between devices, body(): up_whole = lax.all_gather(up_tiles, 'fsdp', axis=0, tiled=True)  32.7 us
    all_gather x1, waiting for transfers between devices, body(): down_whole = lax.all_gather(down_tiles, 'fsdp', axis=0, tiled=True)  31.7 us
    all_gather x1, waiting for transfers between devices, body(): full_input = lax.all_gather(activations, 'tensor', axis=1, tiled=True)  28 us
  transfers between devices with their start and end apart: 9, of which 8 were waited for; matrix products, arithmetic and copies ran while one was open for 34% of the time, Pallas kernels for 0%

commit v1 on v0

--- a/solution.py
+++ b/solution.py
@@ -96,7 +96,7 @@
         ).astype(jnp.float32),
     )
     up_grad, down_grad = (
-        lax.psum(up_part.astype(jnp.bfloat16), "dp").astype(jnp.float32),
+        jnp.sum(lax.all_gather(up_part.astype(jnp.bfloat16), "dp"), axis=0).astype(jnp.float32),
         lax.psum(down_part.astype(jnp.bfloat16), "dp").astype(jnp.float32),
     )
     return (output, input_grad, up_grad, down_grad)

time: 482 us -> 457 us (0.948)
  waiting for transfers between devices: 279 us -> 249 us
  blocking collectives: 0 us -> 7.6 us
    reduce_scatter x1, waiting for transfers between devices: 0.02 us -> 70.8 us  [body(): lax.psum_scatter(up_term.astype(jnp.bfloat16), 'fsdp', scatter_dimension=...]
    reduce_scatter x1, waiting for transfers between devices: 41.9 us -> 0.02 us  [body(): lax.psum_scatter(partial_out.astype(jnp.bfloat16), 'tensor', scatter_dime...]
    reduce_scatter x1, waiting for transfers between devices: 16.4 us -> 0.02 us  [body(): lax.psum_scatter(down_term.astype(jnp.bfloat16), 'fsdp', scatter_dimensio...]
    all_gather x1, waiting for transfers between devices: 31.7 us -> 16.1 us  [body(): down_whole = lax.all_gather(down_tiles, 'fsdp', axis=0, tiled=True)]
    psum x1, waiting for transfers between devices: 45.7 us -> 31.8 us  [body(): lax.psum(down_part.astype(jnp.bfloat16), 'dp').astype(jnp.float32)]
    reduce_scatter x1, waiting for transfers between devices: 42.2 us -> 29.3 us  [body(): lax.psum_scatter(partial_in.astype(jnp.bfloat16), 'tensor', scatter_dimen...]
    all_gather x0 -> x1, blocking collectives: none -> 7.6 us  [body(): lax.all_gather(up_part.astype(jnp.bfloat16), 'dp')]
  transfers between devices with their start and end apart: 9 -> 9, of which waited for: 8 -> 7; matrix products, arithmetic and copies ran while one was open for 34% -> 40% of each run, Pallas kernels for 0% -> 0%
where the time goes in v1:
time: 457 us; the launch traced here: 456 us
  waiting for transfers between devices  249 us (54%)
  local copies, waits for them, and re-layouts  81.3 us (18%)
  other arithmetic  72.9 us (16%)
  matrix products  30.2 us (7%)
  between operations  14 us (3%)
  blocking collectives  7.6 us (2%)
    reduce_scatter x1, waiting for transfers between devices, body(): lax.psum_scatter(up_term.astype(jnp.bfloat16), 'fsdp', scatter_dimension=...  70.8 us
    scatter-add x2, other arithmetic, add_far(): jnp.zeros((rows_here, model_blocks, block_size), jnp.float32)  53.5 us
    all_gather x1, waiting for transfers between devices, body(): full_cotangent = lax.all_gather(cotangent, 'tensor', axis=1, tiled=True)  38.8 us
    all_gather x1, waiting for transfers between devices, body(): up_whole = lax.all_gather(up_tiles, 'fsdp', axis=0, tiled=True)  32.7 us
    psum x1, waiting for transfers between devices, body(): lax.psum(down_part.astype(jnp.bfloat16), 'dp').astype(jnp.float32)  31.8 us
    reduce_scatter x1, waiting for transfers between devices, body(): lax.psum_scatter(partial_in.astype(jnp.bfloat16), 'tensor', scatter_dimen...  29.3 us
    all_gather x1, waiting for transfers between devices, body(): full_input = lax.all_gather(activations, 'tensor', axis=1, tiled=True)  27.5 us
    reshape x2, local copies, waits for them, and re-layouts, add_far(): flat = product.reshape(rows_here, -1, block_size)  18.1 us
  transfers between devices with their start and end apart: 9, of which 7 were waited for; matrix products, arithmetic and copies ran while one was open for 40% of the time, Pallas kernels for 0%

profile of v1, /device:TPU:1, one launch (start us, length us, event | category | flops | bytes accessed | tf_op | source)
XLA Modules:
  0.0 455.7 jit_solution(8221388175862385165)
XLA Ops:
  7.2 1.8 copy.58
  9.1 1.8 copy.65
  11.0 0.7 all-gather.8.cloned.1.call-update
  11.7 0.5 all-gather.6.cloned.1.call-update
  12.3 3.2 sort.62
  15.5 2.5 sort.65
  18.0 3.2 sort.63
  21.2 1.2 gather_fusion.3
  22.5 1.6 gather_fusion
  24.1 27.5 %all-gather.10.cloned.1.call-done = bf16[128,8192]{0,1:T(8,128)(2,1)} async-done(((bf16[128,1024]{0,1:T(8,128)(2,1)}), bf16[128,8192]{0,1:T(8,128)(2,1)}) %all-gather.10.cloned.1.call-update) | async-done | bytes 2097168 | tf_op jit(solution)/shard_map/all_gather | solution.py:49
  51.6 3.2 copy.59
  54.8 38.8 %all-gather.12.cloned.1.call-done = bf16[128,8192]{0,1:T(8,128)(2,1)} async-done(((bf16[128,1024]{0,1:T(8,128)(2,1)}), bf16[128,8192]{0,1:T(8,128)(2,1)}) %all-gather.12.cloned.1.call-update) | async-done | bytes 2097168 | tf_op jit(solution)/shard_map/all_gather | solution.py:67
  93.7 4.1 copy.66
  97.7 4.6 %gather_fusion.5 = bf16[128,128,128]{2,1,0:T(8,128)(2,1)} fusion(bf16[128,64,128]{2,0,1:T(8,128)(2,1)} %copy.66, s32[1024]{0:T(1024)S(1)} %pad_clamp_fusion.2), kind=kCustom, calls=%fused_computation.5 | custom fusion | bytes 8389120 | tf_op jit(solution)/shard_map/gather | solution.py:20
  102.4 3.0 gather_fusion.4
  105.4 32.7 %all-gather.8.cloned.1.call-done = bf16[128,128,128]{2,1,0:T(8,128)(2,1)} async-done(((bf16[8,128,128]{2,1,0:T(8,128)(2,1)}), bf16[128,128,128]{2,1,0:T(8,128)(2,1)}) %all-gather.8.cloned.1.call-update) | async-done | bytes 4194320 | tf_op jit(solution)/shard_map/all_gather | solution.py:51
  138.1 5.2 %gather_fusion.2 = bf16[128,128,128]{2,1,0:T(8,128)(2,1)} fusion(bf16[128,128,128]{2,1,0:T(8,128)(2,1)} %all-gather.8.cloned.1.call-done, s32[1024]{0:T(1024)S(1)} %pad_clamp_fusion.4), kind=kCustom, calls=%fused_computation.2 | custom fusion | bytes 8389120 | tf_op jit(solution)/shard_map/gather | solution.py:36
  143.3 4.9 %convolution_bitcast_fusion.1 = f32[128,16,128]{0,2,1:T(8,128)S(1)} fusion(bf16[16,8,128,128]{3,2,1,0:T(8,128)(2,1)} %bitcast.77, bf16[128,16,8,128]{3,0,2,1:T(8,128)(2,1)} %bitcast.79), kind=kOutput, calls=%fused_computation.14 | convolution fusion | flops 536870912 | bytes 9437184 | tf_op jit(solution)/shard_map/thkb,hkbc->thc/dot_general | solution.py:53
  148.3 3.5 convolution_convert_fusion
  151.7 6.4 %copy.74 = bf16[128,128,128]{2,1,0:T(8,128)(2,1)} copy(bf16[128,128,128]{1,2,0:T(8,128)(2,1)} %bitcast.90) | data formatting | bytes 8388608 | tf_op jit(solution)/shard_map/reshape | solution.py:87
  158.1 5.3 %gather_fusion.7 = bf16[128,128,128]{2,1,0:T(8,128)(2,1)} fusion(bf16[128,128,128]{2,1,0:T(8,128)(2,1)} %copy.74, s32[1024]{0:T(1024)S(1)} %pad_clamp_fusion), kind=kCustom, calls=%fused_computation.7 | custom fusion | bytes 8389120 | tf_op jit(solution)/shard_map/gather | solution.py:89
  163.7 16.1 %all-gather.6.cloned.1.call-done = bf16[128,128,128]{2,1,0:T(8,128)(2,1)} async-done(((bf16[8,128,128]{2,1,0:T(8,128)(2,1)}), bf16[128,128,128]{2,1,0:T(8,128)(2,1)}) %all-gather.6.cloned.1.call-update) | async-done | bytes 4194320 | tf_op jit(solution)/shard_map/all_gather | solution.py:58
  179.8 5.3 %gather_fusion.1 = bf16[128,128,128]{2,1,0:T(8,128)(2,1)} fusion(bf16[128,128,128]{2,1,0:T(8,128)(2,1)} %all-gather.6.cloned.1.call-done, s32[1024]{0:T(1024)S(1)} %pad_clamp_fusion.5), kind=kCustom, calls=%fused_computation.1 | custom fusion | bytes 8389120 | tf_op jit(solution)/shard_map/gather | solution.py:36
  185.1 6.8 %fusion.11 = f32[16,8,128,128]{3,2,1,0:T(8,128)} fusion(bf16[16,8,128,128]{3,2,1,0:T(8,128)(2,1)} %bitcast.87, f32[128,16,128]{0,2,1:T(8,128)S(1)} %convolution_bitcast_fusion.1), kind=kOutput, calls=%fused_computation.39 | convolution fusion | flops 538181632 | bytes 13631488 | tf_op jit(solution)/shard_map/thb,hkbc->thkc/dot_general | solution.py:60
  191.9 9.0 %copy.63 = f32[128,128,128]{2,0,1:T(8,128)} copy(f32[128,128,128]{0,2,1:T(8,128)} %bitcast.84) | data formatting | bytes 16777216 | tf_op jit(solution)/shard_map/reshape | solution.py:27
  201.0 2.5 broadcast.42.clone
  203.4 26.9 %scatter_fusion = f32[128,64,128]{2,0,1:T(8,128)} fusion(f32[128,64,128]{2,0,1:T(8,128)} %broadcast.42.clone, s32[128]{0:T(128)S(1)} %fusion.8, f32[128,128,128]{2,1,0:T(8,128)} %bitcast.82), kind=kCustom, calls=%fused_computation.8 | custom fusion | flops 2097152 | bytes 25166336 | tf_op jit(solution)/shard_map/scatter-add | solution.py:29
  230.3 2.6 convert_element_type.44
  232.9 2.9 copy.64
  235.9 5.1 %fusion.2 = bf16[128,16,128,1]{0,2,3,1:T(8,128)(2,1)S(1)} fusion(bf16[16,8,128,128]{3,2,1,0:T(8,128)(2,1)} %bitcast.88, bf16[128,16,8,128]{3,0,2,1:T(8,128)(2,1)} %bitcast.85, f32[128,16,128]{0,2,1:T(8,128)S(1)} %convolution_bitcast_fusion.1), kind=kOutput, calls=%fused_computation.17 | convolution fusion | flops 539492352 | bytes 9961472 | tf_op jit(solution)/shard_map/thkc,hkbc->thb/dot_general | solution.py:69
  241.0 4.5 fusion.13
  245.4 9.0 %copy.68 = f32[128,128,128]{2,0,1:T(8,128)} copy(f32[128,128,128]{0,2,1:T(8,128)} %bitcast.83) | data formatting | bytes 16777216 | tf_op jit(solution)/shard_map/reshape | solution.py:27
  254.5 2.5 broadcast.42.clone.1
  256.9 26.6 %scatter_fusion.1 = f32[128,64,128]{2,0,1:T(8,128)} fusion(f32[128,64,128]{2,0,1:T(8,128)} %broadcast.42.clone.1, s32[128]{0:T(128)S(1)} %fusion.9, f32[128,128,128]{2,1,0:T(8,128)} %bitcast.81), kind=kCustom, calls=%fused_computation.9 | custom fusion | flops 2097152 | bytes 25166336 | tf_op jit(solution)/shard_map/scatter-add | solution.py:29
  283.6 2.6 convert_element_type.47
  286.2 3.0 copy.69
  289.2 2.5 sort.64
  291.8 5.5 %convolution_convert_fusion.1 = bf16[16,8,128,128]{3,2,1,0:T(8,128)(2,1)} fusion(bf16[128,16,8,128]{3,0,2,1:T(8,128)(2,1)} %bitcast.80, bf16[128,16,128,1]{0,2,3,1:T(8,128)(2,1)S(1)} %fusion.2), kind=kOutput, calls=%fused_computation.11 | convolution fusion | flops 538968064 | bytes 8912896 | tf_op jit(solution)/shard_map/thkb,thc->hkbc/dot_general | solution.py:80
  297.3 5.2 %gather_fusion.6 = bf16[128,128,128]{2,1,0:T(8,128)(2,1)} fusion(bf16[128,128,128]{2,1,0:T(8,128)(2,1)} %bitcast.89, s32[1024]{0:T(1024)S(1)} %pad_clamp_fusion.1), kind=kCustom, calls=%fused_computation.6 | custom fusion | bytes 8389120 | tf_op jit(solution)/shard_map/gather | solution.py:88
  302.6 0.7 all-reduce.2.cloned.1.call-update
  303.3 1.8 copy.75
  305.1 29.3 %reduce-scatter.7.cloned.1.call-done = bf16[128,1024]{0,1:T(8,128)(2,1)} async-done(((bf16[128,8192]{0,1:T(8,128)(2,1)}), bf16[128,1024]{0,1:T(8,128)(2,1)}) %reduce-scatter.7.cloned.1.call-update) | async-done | bytes 262160 | tf_op jit(solution)/shard_map/reduce_scatter | solution.py:77
  334.4 1.8 copy.76
  336.2 70.8 %reduce-scatter.9.cloned.1.call-done = bf16[8,128,128]{2,1,0:T(8,128)(2,1)} async-done(((bf16[128,128,128]{2,1,0:T(8,128)(2,1)}), bf16[8,128,128]{2,1,0:T(8,128)(2,1)}) %reduce-scatter.9.cloned.1.call-update) | async-done | bytes 262160 | tf_op jit(solution)/shard_map/reduce_scatter | solution.py:91
  407.0 7.6 %all-gather = bf16[16,128,128]{2,1,0:T(8,128)(2,1)S(1)} all-gather(bf16[8,128,128]{2,1,0:T(8,128)(2,1)} %reduce-scatter.9.cloned.1.call-done), channel_id=2, replica_groups=mesh['dp'=2,'fsdp'=16,'tensor'=8] {'dp'}, dimensions={0}, use_global_device_ids=true | all-gather | bytes 786432 | tf_op jit(solution)/shard_map/all_gather | solution.py:99
  414.8 0.8 convert_element_type.50
  415.6 31.8 %all-reduce.2.cloned.1.call-done = bf16[8,128,128]{2,1,0:T(8,128)(2,1)} async-done(((bf16[8,128,128]{2,1,0:T(8,128)(2,1)}), bf16[8,128,128]{2,1,0:T(8,128)(2,1)}) %all-reduce.2.cloned.1.call-update) | async-done | bytes 262160 | tf_op jit(solution)/shard_map/psum | solution.py:100
  447.4 1.8 convert_element_type.53
  (42 shorter events, 0.9 us)
Async XLA Ops:
  7.2 14.0 %copy-start = (s32[128,1]{0,1:T(1,128)S(1)}, s32[128,1]{0,1:T(1,128)}, u32[]{:S(2)}) copy-start(s32[128,1]{0,1:T(1,128)} %param.12) | copy-start | bytes 1540
  7.2 44.4 %all-gather.10.cloned.1.call-start = ((), (), s32[]{:S(2)}) async-start(), calls=%async_computation.6 | async-start | bytes 2359296 | tf_op jit(solution)/shard_map/all_gather | solution.py:49
  9.0 84.6 %all-gather.12.cloned.1.call-start = ((), (), s32[]{:S(2)}) async-start(), calls=%async_computation.8 | async-start | bytes 2359296 | tf_op jit(solution)/shard_map/all_gather | solution.py:67
  10.9 127.2 %all-gather.8.cloned.1.call-start = ((), (), s32[]{:S(2)}) async-start(), calls=%async_computation.5 | async-start | bytes 4456448 | tf_op jit(solution)/shard_map/all_gather | solution.py:51
  11.7 168.2 %all-gather.6.cloned.1.call-start = ((), (), s32[]{:S(2)}) async-start(), calls=%async_computation.4 | async-start | bytes 4456448 | tf_op jit(solution)/shard_map/all_gather | solution.py:58
  12.2 290.4 %reduce-scatter.11.cloned.1.call-start = ((), (), s32[]{:S(2)}) async-start(), calls=%async_computation.11 | async-start | bytes 4456448 | tf_op jit(solution)/shard_map/reduce_scatter | solution.py:94
  143.3 4.9 %copy-start.3 = (bf16[128,128,128]{2,1,0:T(8,128)(2,1)S(1)}, bf16[128,128,128]{2,1,0:T(8,128)(2,1)}, u32[]{:S(2)}) copy-start(bf16[128,128,128]{2,1,0:T(8,128)(2,1)} %gather_fusion.5) | copy-start | bytes 12582916
  163.5 139.8 %reduce-scatter.5.cloned.1.call-start = ((), (), s32[]{:S(2)}) async-start(), calls=%async_computation.7 | async-start | bytes 2359296 | tf_op jit(solution)/shard_map/reduce_scatter | solution.py:64
  235.8 98.6 %reduce-scatter.7.cloned.1.call-start = ((), (), s32[]{:S(2)}) async-start(), calls=%async_computation.9 | async-start | bytes 2359296 | tf_op jit(solution)/shard_map/reduce_scatter | solution.py:77
  235.9 5.1 %copy-start.2 = (bf16[128,128,128]{2,1,0:T(8,128)(2,1)S(1)}, bf16[128,128,128]{2,1,0:T(8,128)(2,1)}, u32[]{:S(2)}) copy-start(bf16[128,128,128]{2,1,0:T(8,128)(2,1)} %gather_fusion.2) | copy-start | bytes 12582916
  289.2 117.9 %reduce-scatter.9.cloned.1.call-start = ((), (), s32[]{:S(2)}) async-start(), calls=%async_computation.10 | async-start | bytes 4456448 | tf_op jit(solution)/shard_map/reduce_scatter | solution.py:91
  302.5 146.6 %copy-start.1 = (s32[128,1]{0,1:T(1,128)S(1)}, s32[128,1]{0,1:T(1,128)}, u32[]{:S(2)}) copy-start(s32[128,1]{0,1:T(1,128)} %param.12) | copy-start | bytes 1540
  302.5 144.8 %all-reduce.2.cloned.1.call-start = ((), (), s32[]{:S(2)}) async-start(), calls=%async_computation.12 | async-start | bytes 524288 | tf_op jit(solution)/shard_map/psum | solution.py:100
Sparse Core Ops, SparseCore 0:
  10.4 41.1 all-gather.9
  54.0 39.6 all-gather.11
  95.5 42.5 all-gather.7
  139.8 39.9 all-gather.5
  182.2 66.5 reduce-scatter.10
  251.2 39.6 reduce-scatter.4
  293.5 40.8 reduce-scatter.6
  337.0 70.0 reduce-scatter.8
  409.6 37.7 all-reduce.1
